TPU v7x, 32 devices: a whole 2x2x4 slice. The times are simulated.
32 devices in a mesh: grp: 4 (over y, x), tp: 8 (over z, core).
Axes of the slice: x: 2, y: 2, z: 4, core: 2. Of those that a mesh axis runs over, the one named last changes fastest.
Arguments:
- teacher_in: bfloat16 [192, 8192], P('tp', 'grp'), may hold values from -6 to 6
- teacher_gate: bfloat16 [8192, 28672], P('grp', 'tp'), may hold values from -0.0625 to 0.0625
- teacher_up: bfloat16 [8192, 28672], P('grp', 'tp'), may hold values from -0.0625 to 0.0625
- teacher_down: bfloat16 [28672, 8192], P('tp', 'grp'), may hold values from -0.046875 to 0.046875
- student_in: bfloat16 [192, 4096], P('tp', 'grp'), may hold values from -6 to 6
- student_gate: bfloat16 [4096, 14336], P('grp', 'tp'), may hold values from -0.09375 to 0.09375
- student_up: bfloat16 [4096, 14336], P('grp', 'tp'), may hold values from -0.09375 to 0.09375
- student_down: bfloat16 [14336, 4096], P('tp', 'grp'), may hold values from -0.046875 to 0.046875
- projector: bfloat16 [4096, 4, 2048], P('grp', None, 'tp'), may hold values from -0.09375 to 0.09375
Outputs:
- grad_input: float32 [192, 4096], P('tp', 'grp')
- grad_gate: float32 [4096, 14336], P('grp', 'tp')
- grad_up: float32 [4096, 14336], P('grp', 'tp')
- grad_down: float32 [14336, 4096], P('tp', 'grp')
- grad_projector: float32 [4096, 4, 2048], P('grp', None, 'tp')
All inputs are finite; a program needn't handle non-finite values.
Results may differ from a plain program's by a relative error of at most 0.017.
Values may be sent and summed in bfloat16 or wider, within the bound.
No kernel may reach another device: no remote copies, remote signals or barrier semaphores. Data moves between devices by JAX's collectives and lax.ppermute only.
A program may use at most 192 MiB of HBM per device.

v0:
```python
import jax
import jax.numpy as jnp
from jax import lax
from jax.sharding import PartitionSpec as P


def body(
    teacher_in,
    teacher_gate,
    teacher_up,
    teacher_down,
    student_in,
    student_gate,
    student_up,
    student_down,
    projector,
):
    bf = jnp.bfloat16
    fl = jnp.float32
    teacher_pair = jnp.concatenate([teacher_gate, teacher_up], axis=1)
    teacher_width = teacher_gate.shape[1]
    teacher_partial = jnp.dot(
        lax.all_gather(teacher_in, "tp", axis=0, tiled=True),
        teacher_pair,
        preferred_element_type=fl,
    )
    teacher_pre = lax.psum_scatter(teacher_partial, "grp", scatter_dimension=0, tiled=True)
    teacher_hidden = (
        jax.nn.silu(teacher_pre[:, :teacher_width]) * teacher_pre[:, teacher_width:]
    ).astype(bf)
    teacher_sums = jnp.dot(
        lax.all_gather(teacher_hidden, "grp", axis=0, tiled=True),
        teacher_down,
        preferred_element_type=fl,
    )
    teacher_share = lax.psum_scatter(teacher_sums, "tp", scatter_dimension=1, tiled=True)
    teacher_feature = lax.all_to_all(
        teacher_share.astype(bf), "grp", split_axis=0, concat_axis=1, tiled=True
    )
    student_pair = jnp.concatenate([student_gate, student_up], axis=1)
    student_width = student_gate.shape[1]
    input_rows = lax.all_gather(student_in, "tp", axis=0, tiled=True)
    student_partial = jnp.dot(input_rows, student_pair, preferred_element_type=fl)
    student_pre = lax.psum_scatter(student_partial, "grp", scatter_dimension=0, tiled=True)
    gate_values = student_pre[:, :student_width]
    up_values = student_pre[:, student_width:]
    student_hidden = (jax.nn.silu(gate_values) * up_values).astype(bf)
    hidden_rows = lax.all_gather(student_hidden, "grp", axis=0, tiled=True)
    feature_sum = lax.psum(jnp.dot(hidden_rows, student_down, preferred_element_type=fl), "tp")
    student_feature = feature_sum.astype(bf)
    proj_matrix = projector.reshape(projector.shape[0], -1)
    projected = lax.psum_scatter(
        jnp.dot(student_feature, proj_matrix, preferred_element_type=fl),
        "grp",
        scatter_dimension=0,
        tiled=True,
    )
    residual_grad = (projected - teacher_feature.astype(fl)).astype(bf)
    residual_rows = lax.all_gather(residual_grad, "grp", axis=0, tiled=True)
    grad_projector = jnp.dot(student_feature.T, residual_rows, preferred_element_type=fl).reshape(
        projector.shape
    )
    feature_grad = lax.psum(
        jnp.dot(residual_rows, proj_matrix.T, preferred_element_type=fl), "tp"
    ).astype(bf)
    grad_down = jnp.dot(hidden_rows.T, feature_grad, preferred_element_type=fl)
    hidden_grad = lax.psum_scatter(
        jnp.dot(feature_grad, student_down.T, preferred_element_type=fl),
        "grp",
        scatter_dimension=0,
        tiled=True,
    )
    sigmoid_gate = jax.nn.sigmoid(gate_values)
    gate_grad = (
        hidden_grad * up_values * sigmoid_gate * (1.0 + gate_values * (1.0 - sigmoid_gate))
    ).astype(bf)
    up_grad = (hidden_grad * gate_values * sigmoid_gate).astype(bf)
    pair_rows = lax.all_gather(
        jnp.concatenate([gate_grad, up_grad], axis=1), "grp", axis=0, tiled=True
    )
    grad_pair = jnp.dot(input_rows.T, pair_rows, preferred_element_type=fl)
    grad_input = lax.psum_scatter(
        jnp.dot(pair_rows, student_pair.T, preferred_element_type=fl).astype(jnp.bfloat16),
        "tp",
        scatter_dimension=0,
        tiled=True,
    ).astype(jnp.float32)
    return (
        grad_input,
        grad_pair[:, :student_width],
        grad_pair[:, student_width:],
        grad_down,
        grad_projector,
    )


def solution(mesh):
    placed = (
        P("tp", "grp"),
        P("grp", "tp"),
        P("grp", "tp"),
        P("tp", "grp"),
        P("tp", "grp"),
        P("grp", "tp"),
        P("grp", "tp"),
        P("tp", "grp"),
        P("grp", None, "tp"),
    )
    return jax.shard_map(
        body,
        mesh=mesh,
        in_specs=placed,
        out_specs=(
            P("tp", "grp"),
            P("grp", "tp"),
            P("grp", "tp"),
            P("tp", "grp"),
            P("grp", None, "tp"),
        ),
        check_vma=False,
    )
```

profile of v0, /device:TPU:0, one launch (start us, length us, event | category | flops | bytes accessed | tf_op | source)
XLA Modules:
  0.0 422.7 jit_solution(930207206825908747)
XLA Ops:
  7.2 17.4 %all_gather.20 = bf16[192,2048]{1,0:T(8,128)(2,1)S(1)} all-gather(bf16[24,2048]{1,0:T(8,128)(2,1)} %param.9), channel_id=1, replica_groups=mesh['grp'=4,'tp'=8] {'tp'}, dimensions={0}, use_global_device_ids=true | all-gather | bytes 884736 | tf_op jit(solution)/shard_map/all_gather | solution.py:23
  24.6 14.3 %fusion.4 = f32[192,7168]{1,0:T(8,128)} fusion(bf16[192,2048]{1,0:T(8,128)(2,1)S(1)} %all_gather.20, bf16[2048,3584]{1,0:T(8,128)(2,1)} %param.11, bf16[2048,3584]{1,0:T(8,128)(2,1)} %param.10), kind=kOutput, calls=%fused_computation.4 | convolution fusion | flops 5695864832 | bytes 35651584 | tf_op jit(solution)/shard_map/dot_general | solution.py:22
  39.0 64.8 %reduce-scatter.11.cloned.1.call-done = f32[48,7168]{1,0:T(8,128)} async-done(((f32[192,7168]{1,0:T(8,128)}), f32[48,7168]{1,0:T(8,128)}) %reduce-scatter.11.cloned.1.call-update) | async-done | bytes 1376272 | tf_op jit(solution)/shard_map/reduce_scatter | solution.py:27
  103.8 2.2 fusion.7
  106.1 14.6 %all_gather.18 = bf16[192,1024]{1,0:T(8,128)(2,1)S(1)} all-gather(bf16[24,1024]{1,0:T(8,128)(2,1)S(1)} %copy-done.8), channel_id=1, replica_groups=mesh['grp'=4,'tp'=8] {'tp'}, dimensions={0}, use_global_device_ids=true | all-gather | bytes 442368 | tf_op jit(solution)/shard_map/all_gather | solution.py:42
  120.7 2.5 constant_dynamic-update-slice_fusion.1
  123.5 3.0 copy-done
  126.6 3.1 convolution_bitcast_fusion.1
  129.8 5.7 %all-gather.3.cloned.1.call-done = bf16[192,3584]{1,0:T(8,128)(2,1)} async-done(((bf16[48,3584]{1,0:T(8,128)(2,1)}), bf16[192,3584]{1,0:T(8,128)(2,1)}) %all-gather.3.cloned.1.call-update) | async-done | bytes 1376272 | tf_op jit(solution)/shard_map/all_gather | solution.py:32
  135.4 9.8 %fusion.19 = f32[192,2048]{1,0:T(8,128)} fusion(bf16[192,3584]{1,0:T(8,128)(2,1)} %all-gather.3.cloned.1.call-done, bf16[3584,2048]{1,0:T(8,128)(2,1)} %param.12), kind=kOutput, calls=%fused_computation.30 | convolution fusion | flops 2818572288 | bytes 17629184 | tf_op jit(solution)/shard_map/dot_general | solution.py:31
  145.3 2.2 copy.23
  147.4 32.3 %reduce-scatter.7.cloned.1.call-done = f32[48,3584]{1,0:T(8,128)} async-done(((f32[192,3584]{1,0:T(8,128)}), f32[48,3584]{1,0:T(8,128)}) %reduce-scatter.7.cloned.1.call-update) | async-done | bytes 688144 | tf_op jit(solution)/shard_map/reduce_scatter | solution.py:44
  180.9 10.7 %all_gather.19 = bf16[192,1792]{1,0:T(8,128)(2,1)S(1)} all-gather(bf16[48,1792]{1,0:T(8,128)(2,1)S(1)} %multiply_convert_fusion.2), channel_id=1, replica_groups=mesh['grp'=4,'tp'=8] {'grp'}, dimensions={0}, use_global_device_ids=true | all-gather | bytes 860160 | tf_op jit(solution)/shard_map/all_gather | solution.py:48
  191.6 3.8 fusion.18
  195.4 38.1 %all-reduce.2 = bf16[192,1024]{1,0:T(8,128)(2,1)S(1)} all-reduce(f32[192,1024]{1,0:T(8,128)} %fusion.18), channel_id=1, replica_groups=mesh['grp'=4,'tp'=8] {'tp'}, use_global_device_ids=true, to_apply=%region_1.2 | all-reduce | flops 196608 | bytes 1179648 | tf_op jit(solution)/shard_map/psum | solution.py:49
  233.5 1.5 fusion.24
  236.1 7.8 %all_to_all.13 = bf16[4,48,256]{2,1,0:T(8,128)(2,1)S(1)} all-to-all(bf16[4,48,256]{2,1,0:T(8,128)(2,1)S(1)} %bitcast.40), channel_id=1, replica_groups=mesh['grp'=4,'tp'=8] {'grp'}, dimensions={0} | all-to-all | bytes 196608 | tf_op jit(solution)/shard_map/all_to_all | solution.py:37
  243.9 14.5 %reduce-scatter.9.cloned.1.call-done = f32[48,1024]{1,0:T(8,128)} async-done(((f32[192,1024]{1,0:T(8,128)}), f32[48,1024]{1,0:T(8,128)}) %reduce-scatter.9.cloned.1.call-update) | async-done | bytes 196624 | tf_op jit(solution)/shard_map/reduce_scatter | solution.py:52
  259.4 9.6 %all_gather.22 = bf16[192,1024]{1,0:T(8,128)(2,1)S(1)} all-gather(bf16[48,1024]{1,0:T(8,128)(2,1)S(1)} %subtract_convert_fusion), channel_id=1, replica_groups=mesh['grp'=4,'tp'=8] {'grp'}, dimensions={0}, use_global_device_ids=true | all-gather | bytes 491520 | tf_op jit(solution)/shard_map/all_gather | solution.py:59
  269.7 1.7 fusion.20
  271.4 35.0 %all-reduce.3 = bf16[192,1024]{1,0:T(8,128)(2,1)S(1)} all-reduce(f32[192,1024]{1,0:T(8,128)} %fusion.20), channel_id=1, replica_groups=mesh['grp'=4,'tp'=8] {'tp'}, use_global_device_ids=true, to_apply=%region_5.6 | all-reduce | flops 196608 | bytes 1179648 | tf_op jit(solution)/shard_map/psum | solution.py:63
  306.4 4.5 %fusion.22 = f32[192,1792]{1,0:T(8,128)} fusion(bf16[192,1024]{1,0:T(8,128)(2,1)S(1)} %all-reduce.3, bf16[1792,1024]{1,0:T(8,128)(2,1)} %param.16), kind=kOutput, calls=%fused_computation.33 | convolution fusion | flops 704643072 | bytes 5439488 | tf_op jit(solution)/shard_map/dot_general | solution.py:68
  311.1 27.0 %reduce-scatter.15.cloned.1.call-done = f32[48,1792]{1,0:T(8,128)} async-done(((f32[192,1792]{1,0:T(8,128)}), f32[48,1792]{1,0:T(8,128)}) %reduce-scatter.15.cloned.1.call-update) | async-done | bytes 344080 | tf_op jit(solution)/shard_map/reduce_scatter | solution.py:67
  340.1 2.8 fusion.23
  342.9 5.3 %copy.21 = f32[1024,4,256]{2,1,0:T(4,128)} copy(f32[1024,4,256]{0,2,1:T(8,128)} %bitcast.35) | data formatting | bytes 8388608
  348.2 4.2 fusion.21
  352.4 17.1 %all-gather.5.cloned.1.call-done = bf16[192,3584]{1,0:T(8,128)(2,1)} async-done(((bf16[48,3584]{1,0:T(8,128)(2,1)}), bf16[192,3584]{1,0:T(8,128)(2,1)}) %all-gather.5.cloned.1.call-update) | async-done | bytes 1376272 | tf_op jit(solution)/shard_map/all_gather | solution.py:78
  369.4 6.9 %convolution_convert_fusion = bf16[192,1024]{1,0:T(8,128)(2,1)} fusion(bf16[192,3584]{1,0:T(8,128)(2,1)} %all-gather.5.cloned.1.call-done, bf16[1024,3584]{1,0:T(8,128)(2,1)} %copy-done), kind=kOutput, calls=%fused_computation.7 | convolution fusion | flops 1409482752 | bytes 9109504 | tf_op jit(solution)/shard_map/dot_general | solution.py:83
  376.4 7.3 %convolution_bitcast_fusion = f32[1024,3584]{0,1:T(8,128)} fusion(bf16[192,3584]{1,0:T(8,128)(2,1)S(1)} %copy-done.7, bf16[192,1024]{1,0:T(8,128)(2,1)S(1)} %copy-done.2), kind=kOutput, calls=%fused_computation.5 | convolution fusion | flops 1409286144 | bytes 16449536 | tf_op jit(solution)/shard_map/dot_general | solution.py:81
  383.7 13.9 %fusion.17 = (f32[1024,1792]{0,1:T(8,128)}, f32[1024,1792]{0,1:T(8,128)}) fusion(f32[1024,3584]{0,1:T(8,128)} %convolution_bitcast_fusion), kind=kLoop, calls=%fused_computation.28 | loop fusion | bytes 29360128 | tf_op jit(solution)/shard_map/slice | solution.py:91
  397.6 8.4 %copy.19 = f32[1024,1792]{1,0:T(8,128)} copy(f32[1024,1792]{0,1:T(8,128)} %get-tuple-element.16) | data formatting | bytes 14680064
  406.0 8.4 %copy.20 = f32[1024,1792]{1,0:T(8,128)} copy(f32[1024,1792]{0,1:T(8,128)} %get-tuple-element.15) | data formatting | bytes 14680064
  (44 shorter events, 8.2 us)
Async XLA Ops:
  7.2 96.6 %reduce-scatter.11.cloned.1.call-start = ((), (), s32[]{:S(2)}) async-start(), calls=%async_computation.9 | async-start | bytes 6881280 | tf_op jit(solution)/shard_map/reduce_scatter | solution.py:27
  38.9 67.1 %copy-start.8 = (bf16[24,1024]{1,0:T(8,128)(2,1)S(1)}, bf16[24,1024]{1,0:T(8,128)(2,1)}, u32[]{:S(2)}) copy-start(bf16[24,1024]{1,0:T(8,128)(2,1)} %param.13) | copy-start | bytes 147460
  39.0 96.5 %all-gather.3.cloned.1.call-start = ((), (), s32[]{:S(2)}) async-start(), calls=%async_computation.10 | async-start | bytes 1720320 | tf_op jit(solution)/shard_map/all_gather | solution.py:32
  106.0 73.7 %reduce-scatter.7.cloned.1.call-start = ((), (), s32[]{:S(2)}) async-start(), calls=%async_computation.7 | async-start | bytes 3440640 | tf_op jit(solution)/shard_map/reduce_scatter | solution.py:44
  106.1 17.1 %copy-start.3 = (bf16[1024,1792]{1,0:T(8,128)(2,1)S(1)}, bf16[1024,1792]{1,0:T(8,128)(2,1)}, u32[]{:S(2)}) copy-start(bf16[1024,1792]{1,0:T(8,128)(2,1)} %param.15) | copy-start | bytes 11010052
  120.7 2.8 copy-start.1
  123.5 3.1 copy-start
  129.7 105.4 %reduce-scatter.13.cloned.1.call-start = ((), (), s32[]{:S(2)}) async-start(), calls=%async_computation.11 | async-start | bytes 1769472 | tf_op jit(solution)/shard_map/reduce_scatter | solution.py:36
  145.2 113.2 %reduce-scatter.9.cloned.1.call-start = ((), (), s32[]{:S(2)}) async-start(), calls=%async_computation.8 | async-start | bytes 983040 | tf_op jit(solution)/shard_map/reduce_scatter | solution.py:52
  235.0 103.1 %reduce-scatter.15.cloned.1.call-start = ((), (), s32[]{:S(2)}) async-start(), calls=%async_computation.12 | async-start | bytes 1720320 | tf_op jit(solution)/shard_map/reduce_scatter | solution.py:67
  268.9 0.7 copy-start.4
  271.4 66.8 %copy-start.6 = (f32[48,3584]{1,0:T(8,128)S(1)}, f32[48,3584]{1,0:T(8,128)}, u32[]{:S(2)}) copy-start(f32[48,3584]{1,0:T(8,128)} %reduce-scatter.7.cloned.1.call-done) | copy-start | bytes 2064388
  271.4 68.7 %copy-start.5 = (bf16[192,1024]{1,0:T(8,128)(2,1)S(1)}, bf16[192,1024]{1,0:T(8,128)(2,1)}, u32[]{:S(2)}) copy-start(bf16[192,1024]{1,0:T(8,128)(2,1)} %copy-done.4) | copy-start | bytes 1179652
  310.9 58.5 %all-gather.5.cloned.1.call-start = ((), (), s32[]{:S(2)}) async-start(), calls=%async_computation.13 | async-start | bytes 1720320 | tf_op jit(solution)/shard_map/all_gather | solution.py:78
  340.1 74.3 %reduce-scatter.17.cloned.1.call-start = ((), (), s32[]{:S(2)}) async-start(), calls=%async_computation.14 | async-start | bytes 442368 | tf_op jit(solution)/shard_map/reduce_scatter | solution.py:82
  352.4 24.0 %copy-start.2 = (bf16[192,1024]{1,0:T(8,128)(2,1)S(1)}, bf16[192,1024]{1,0:T(8,128)(2,1)}, u32[]{:S(2)}) copy-start(bf16[192,1024]{1,0:T(8,128)(2,1)} %copy-done.1) | copy-start | bytes 1179652
  369.4 6.9 %copy-start.7 = (bf16[192,3584]{1,0:T(8,128)(2,1)S(1)}, bf16[192,3584]{1,0:T(8,128)(2,1)}, u32[]{:S(2)}) copy-start(bf16[192,3584]{1,0:T(8,128)(2,1)} %all-gather.5.cloned.1.call-done) | copy-start | bytes 4128772
Sparse Core Ops, SparseCore 0:
  39.1 64.6 reduce-scatter.10
  106.2 29.1 all-gather.2
  139.0 40.6 reduce-scatter.6
  182.4 36.0 reduce-scatter.12
  235.2 23.2 reduce-scatter.8
  311.0 27.0 reduce-scatter.14
  340.2 29.1 all-gather.4
  376.5 31.1 reduce-scatter.16
where the time goes:
time: 424 us; the launch traced here: 423 us
  waiting for transfers between devices  161 us (38%)
  blocking collectives  133 us (31%)
  matrix products  59.9 us (14%)
  local copies, waits for them, and re-layouts  44.7 us (11%)
  between operations  14.3 us (3%)
  other arithmetic  8.64 us (2%)
    reduce_scatter x1, waiting for transfers between devices, body(): lax.psum_scatter(teacher_partial, 'grp', scatter_dimension=0, tiled=True)  64.8 us
    psum x1, blocking collectives, body(): lax.psum(jnp.dot(hidden_rows, student_down, preferred_element_type=fl), '...  38.1 us
    psum x1, blocking collectives, body(): lax.psum(jnp.dot(residual_rows, proj_matrix.T, preferred_element_type=fl)...  35 us
    reduce_scatter x1, waiting for transfers between devices, body(): lax.psum_scatter(student_partial, 'grp', scatter_dimension=0, tiled=True)  32.3 us
    unnamed x23, local copies, waits for them, and re-layouts  30.4 us
    reduce_scatter x1, waiting for transfers between devices, body(): lax.psum_scatter(jnp.dot(feature_grad, student_down.T, preferred_element_...  27 us
    all_gather x1, blocking collectives, body(): lax.all_gather(teacher_in, 'tp', axis=0, tiled=True)  17.4 us
    all_gather x1, waiting for transfers between devices, body(): lax.all_gather(jnp.concatenate([gate_grad, up_grad], axis=1), 'grp', axis...  17.1 us
  transfers between devices with their start and end apart: 8, of which 6 were waited for; matrix products, arithmetic and copies ran while one was open for 18% of the time, Pallas kernels for 0%

commit v1 on v0

--- a/solution.py
+++ b/solution.py
@@ -2,6 +2,22 @@
 import jax.numpy as jnp
 from jax import lax
 from jax.sharding import PartitionSpec as P
+
+
+def ring_gather(x, axis, dim):
+    ways, here, lap = (lax.axis_size(axis), lax.axis_index(axis), x.shape[dim])
+    lengths = [n * ways if d == dim else n for d, n in enumerate(x.shape)]
+    full = lax.dynamic_update_slice_in_dim(jnp.zeros(lengths, x.dtype), x, here * lap, axis=dim)
+    going_up = going_down = x
+    for far in range(1, ways // 2 + 1):
+        going_up = lax.ppermute(going_up, axis, [(d, (d + 1) % ways) for d in range(ways)])
+        full = lax.dynamic_update_slice_in_dim(full, going_up, (here - far) % ways * lap, axis=dim)
+        if 2 * far < ways:
+            going_down = lax.ppermute(going_down, axis, [(d, (d - 1) % ways) for d in range(ways)])
+            full = lax.dynamic_update_slice_in_dim(
+                full, going_down, (here + far) % ways * lap, axis=dim
+            )
+    return full
 
 
 def body(
@@ -39,7 +55,7 @@
     )
     student_pair = jnp.concatenate([student_gate, student_up], axis=1)
     student_width = student_gate.shape[1]
-    input_rows = lax.all_gather(student_in, "tp", axis=0, tiled=True)
+    input_rows = ring_gather(student_in, "tp", 0)
     student_partial = jnp.dot(input_rows, student_pair, preferred_element_type=fl)
     student_pre = lax.psum_scatter(student_partial, "grp", scatter_dimension=0, tiled=True)
     gate_values = student_pre[:, :student_width]

time: 424 us -> 417 us (0.983)
  local copies, waits for them, and re-layouts: 44.7 us -> 27 us
  blocking collectives: 133 us -> 119 us
  waiting for transfers between devices: 161 us -> 173 us
  starting transfers between devices: 0.51 us -> 11 us
    unnamed x23 -> x19, local copies, waits for them, and re-layouts: 30.4 us -> 13.2 us
    all_gather x1 -> x0, blocking collectives: 14.6 us -> none  [body(): input_rows = lax.all_gather(student_in, 'tp', axis=0, tiled=True)]
    reduce_scatter x1, waiting for transfers between devices: 0.01 us -> 12.3 us  [body(): lax.psum_scatter(jnp.dot(pair_rows, student_pair.T, preferred_element_typ...]
    ppermute x0 -> x7, starting transfers between devices: none -> 10.7 us  [the longest x3 10.3 us: ring_gather(): lax.ppermute(going_down, axis, [(d, (d - 1) % ways) for d in range(ways)])]
    ppermute x0 -> x7, waiting for transfers between devices: none -> 9.05 us  [the longest x4 9.05 us: ring_gather(): lax.ppermute(going_up, axis, [(d, (d + 1) % ways) for d in range(ways)])]
    all_gather x1, waiting for transfers between devices: 5.65 us -> 0.08 us  [body(): lax.all_gather(teacher_hidden, 'grp', axis=0, tiled=True)]
    reduce_scatter x1, waiting for transfers between devices: 64.8 us -> 60.5 us  [body(): lax.psum_scatter(teacher_partial, 'grp', scatter_dimension=0, tiled=True)]
  transfers between devices with their start and end apart: 8 -> 15, of which waited for: 6 -> 10; matrix products, arithmetic and copies ran while one was open for 18% -> 16% of each run, Pallas kernels for 0% -> 0%
where the time goes in v1:
time: 417 us; the launch traced here: 416 us
  waiting for transfers between devices  173 us (41%)
  blocking collectives  119 us (29%)
  matrix products  63.1 us (15%)
  local copies, waits for them, and re-layouts  27 us (6%)
  between operations  14.5 us (3%)
  starting transfers between devices  11 us (3%)
  other arithmetic  8.64 us (2%)
    reduce_scatter x1, waiting for transfers between devices, body(): lax.psum_scatter(teacher_partial, 'grp', scatter_dimension=0, tiled=True)  60.5 us
    psum x1, blocking collectives, body(): lax.psum(jnp.dot(hidden_rows, student_down, preferred_element_type=fl), '...  38.1 us
    psum x1, blocking collectives, body(): lax.psum(jnp.dot(residual_rows, proj_matrix.T, preferred_element_type=fl)...  35.1 us
    reduce_scatter x1, waiting for transfers between devices, body(): lax.psum_scatter(student_partial, 'grp', scatter_dimension=0, tiled=True)  32.3 us
    reduce_scatter x1, waiting for transfers between devices, body(): lax.psum_scatter(jnp.dot(feature_grad, student_down.T, preferred_element_...  27.2 us
    all_gather x1, blocking collectives, body(): lax.all_gather(teacher_in, 'tp', axis=0, tiled=True)  17.4 us
    all_gather x1, waiting for transfers between devices, body(): lax.all_gather(jnp.concatenate([gate_grad, up_grad], axis=1), 'grp', axis...  17.1 us
    reduce_scatter x1, waiting for transfers between devices, body(): lax.psum_scatter(jnp.dot(student_feature, proj_matrix, preferred_element_...  14.6 us
  transfers between devices with their start and end apart: 15, of which 10 were waited for; matrix products, arithmetic and copies ran while one was open for 16% of the time, Pallas kernels for 0%

profile of v1, /device:TPU:0, one launch (start us, length us, event | category | flops | bytes accessed | tf_op | source)
XLA Modules:
  0.0 416.3 jit_solution(6634452417784411079)
XLA Ops:
  7.2 17.4 %all_gather.16 = bf16[192,2048]{1,0:T(8,128)(2,1)S(1)} all-gather(bf16[24,2048]{1,0:T(8,128)(2,1)} %param.9), channel_id=1, replica_groups=mesh['grp'=4,'tp'=8] {'tp'}, dimensions={0}, use_global_device_ids=true | all-gather | bytes 884736 | tf_op jit(solution)/shard_map/all_gather | solution.py:39
  24.6 14.3 %fusion.4 = f32[192,7168]{1,0:T(8,128)} fusion(bf16[192,2048]{1,0:T(8,128)(2,1)S(1)} %all_gather.16, bf16[2048,3584]{1,0:T(8,128)(2,1)} %param.11, bf16[2048,3584]{1,0:T(8,128)(2,1)} %param.10), kind=kOutput, calls=%fused_computation.4 | convolution fusion | flops 5695864832 | bytes 35651584 | tf_op jit(solution)/shard_map/dot_general | solution.py:38
  40.1 3.2 collective-permute-start.1
  43.3 60.5 %reduce-scatter.11.cloned.1.call-done = f32[48,7168]{1,0:T(8,128)} async-done(((f32[192,7168]{1,0:T(8,128)}), f32[48,7168]{1,0:T(8,128)}) %reduce-scatter.11.cloned.1.call-update) | async-done | bytes 1376272 | tf_op jit(solution)/shard_map/reduce_scatter | solution.py:43
  103.8 2.2 fusion.7
  106.1 4.3 %constant_dynamic-update-slice_fusion.1 = bf16[1024,3584]{1,0:T(8,128)(2,1)} fusion(bf16[1024,1792]{1,0:T(8,128)(2,1)} %param.14), kind=kLoop, calls=%fused_computation.24 | loop fusion | bytes 7340032
  110.4 2.1 constant_dynamic-update-slice_fusion
  112.7 3.5 collective-permute-start.3
  118.1 3.5 collective-permute-start.5
  121.7 1.9 collective-permute-done.4
  123.6 5.3 %collective-permute-done.6 = bf16[24,1024]{1,0:T(8,128)(2,1)S(1)} collective-permute-done((bf16[24,1024]{1,0:T(8,128)(2,1)S(1)}, bf16[24,1024]{1,0:T(8,128)(2,1)S(1)}, u32[]{:S(2)}, u32[]{:S(2)}) %collective-permute-start.6) | collective-permute-done | bytes 49184 | tf_op jit(solution)/shard_map/ppermute | solution.py:13
  128.9 6.4 %fusion.18 = f32[192,3584]{1,0:T(8,128)} fusion(bf16[192,1024]{1,0:T(8,128)(2,1)S(1)} %constant_dynamic-update-slice_fusion.2, bf16[1024,3584]{1,0:T(8,128)(2,1)} %constant_dynamic-update-slice_fusion), kind=kOutput, calls=%fused_computation.35 | convolution fusion | flops 1409286144 | bytes 10485760 | tf_op jit(solution)/shard_map/dot_general | solution.py:59
  135.4 9.8 %fusion.20 = f32[192,2048]{1,0:T(8,128)} fusion(bf16[192,3584]{1,0:T(8,128)(2,1)} %all-gather.3.cloned.1.call-done, bf16[3584,2048]{1,0:T(8,128)(2,1)} %param.12), kind=kOutput, calls=%fused_computation.37 | convolution fusion | flops 2818572288 | bytes 17629184 | tf_op jit(solution)/shard_map/dot_general | solution.py:47
  145.3 2.2 copy.19
  147.4 32.3 %reduce-scatter.7.cloned.1.call-done = f32[48,3584]{1,0:T(8,128)} async-done(((f32[192,3584]{1,0:T(8,128)}), f32[48,3584]{1,0:T(8,128)}) %reduce-scatter.7.cloned.1.call-update) | async-done | bytes 688144 | tf_op jit(solution)/shard_map/reduce_scatter | solution.py:60
  180.9 10.7 %all_gather.15 = bf16[192,1792]{1,0:T(8,128)(2,1)S(1)} all-gather(bf16[48,1792]{1,0:T(8,128)(2,1)S(1)} %multiply_convert_fusion.2), channel_id=1, replica_groups=mesh['grp'=4,'tp'=8] {'grp'}, dimensions={0}, use_global_device_ids=true | all-gather | bytes 860160 | tf_op jit(solution)/shard_map/all_gather | solution.py:64
  191.6 3.8 fusion.19
  195.4 38.1 %all-reduce.2 = bf16[192,1024]{1,0:T(8,128)(2,1)S(1)} all-reduce(f32[192,1024]{1,0:T(8,128)} %fusion.19), channel_id=1, replica_groups=mesh['grp'=4,'tp'=8] {'tp'}, use_global_device_ids=true, to_apply=%region_1.2 | all-reduce | flops 196608 | bytes 1179648 | tf_op jit(solution)/shard_map/psum | solution.py:65
  236.1 7.9 %all_to_all.13 = bf16[4,48,256]{2,1,0:T(8,128)(2,1)S(1)} all-to-all(bf16[4,48,256]{2,1,0:T(8,128)(2,1)S(1)} %bitcast.36), channel_id=1, replica_groups=mesh['grp'=4,'tp'=8] {'grp'}, dimensions={0} | all-to-all | bytes 196608 | tf_op jit(solution)/shard_map/all_to_all | solution.py:53
  244.0 14.6 %reduce-scatter.9.cloned.1.call-done = f32[48,1024]{1,0:T(8,128)} async-done(((f32[192,1024]{1,0:T(8,128)}), f32[48,1024]{1,0:T(8,128)}) %reduce-scatter.9.cloned.1.call-update) | async-done | bytes 196624 | tf_op jit(solution)/shard_map/reduce_scatter | solution.py:68
  259.6 9.6 %all_gather.18 = bf16[192,1024]{1,0:T(8,128)(2,1)S(1)} all-gather(bf16[48,1024]{1,0:T(8,128)(2,1)S(1)} %subtract_convert_fusion), channel_id=1, replica_groups=mesh['grp'=4,'tp'=8] {'grp'}, dimensions={0}, use_global_device_ids=true | all-gather | bytes 491520 | tf_op jit(solution)/shard_map/all_gather | solution.py:75
  271.7 35.1 %all-reduce.3 = bf16[192,1024]{1,0:T(8,128)(2,1)S(1)} all-reduce(f32[192,1024]{1,0:T(8,128)} %fusion.21), channel_id=1, replica_groups=mesh['grp'=4,'tp'=8] {'tp'}, use_global_device_ids=true, to_apply=%region_5.6 | all-reduce | flops 196608 | bytes 1179648 | tf_op jit(solution)/shard_map/psum | solution.py:79
  306.7 4.5 %fusion.24 = f32[192,1792]{1,0:T(8,128)} fusion(bf16[192,1024]{1,0:T(8,128)(2,1)S(1)} %all-reduce.3, bf16[1792,1024]{1,0:T(8,128)(2,1)} %param.16), kind=kOutput, calls=%fused_computation.41 | convolution fusion | flops 704643072 | bytes 5439488 | tf_op jit(solution)/shard_map/dot_general | solution.py:84
  311.3 27.2 %reduce-scatter.15.cloned.1.call-done = f32[48,1792]{1,0:T(8,128)} async-done(((f32[192,1792]{1,0:T(8,128)}), f32[48,1792]{1,0:T(8,128)}) %reduce-scatter.15.cloned.1.call-update) | async-done | bytes 344080 | tf_op jit(solution)/shard_map/reduce_scatter | solution.py:83
  340.6 2.8 fusion.25
  343.3 5.3 %copy.17 = f32[1024,4,256]{2,1,0:T(4,128)} copy(f32[1024,4,256]{0,2,1:T(8,128)} %bitcast.31) | data formatting | bytes 8388608
  348.6 4.2 %fusion.23 = f32[1792,1024]{1,0:T(8,128)} fusion(bf16[192,1792]{1,0:T(8,128)(2,1)S(1)} %all_gather.15, bf16[192,1024]{1,0:T(8,128)(2,1)S(1)} %all-reduce.3), kind=kOutput, calls=%fused_computation.40 | convolution fusion | flops 704643072 | bytes 8421376 | tf_op jit(solution)/shard_map/dot_general | solution.py:82
  352.8 17.1 %all-gather.5.cloned.1.call-done = bf16[192,3584]{1,0:T(8,128)(2,1)} async-done(((bf16[48,3584]{1,0:T(8,128)(2,1)}), bf16[192,3584]{1,0:T(8,128)(2,1)}) %all-gather.5.cloned.1.call-update) | async-done | bytes 1376272 | tf_op jit(solution)/shard_map/all_gather | solution.py:94
  369.9 6.9 %convolution_convert_fusion = bf16[192,1024]{1,0:T(8,128)(2,1)} fusion(bf16[192,3584]{1,0:T(8,128)(2,1)} %all-gather.5.cloned.1.call-done, bf16[1024,3584]{1,0:T(8,128)(2,1)} %constant_dynamic-update-slice_fusion), kind=kOutput, calls=%fused_computation.5 | convolution fusion | flops 1409482752 | bytes 9109504 | tf_op jit(solution)/shard_map/dot_general | solution.py:99
  376.8 7.3 %fusion.22 = f32[1024,3584]{1,0:T(8,128)} fusion(bf16[192,1024]{1,0:T(8,128)(2,1)S(1)} %copy-done.1, bf16[192,3584]{1,0:T(8,128)(2,1)S(1)} %copy-done.6), kind=kOutput, calls=%fused_computation.39 | convolution fusion | flops 1409286144 | bytes 16449536 | tf_op jit(solution)/shard_map/dot_general | solution.py:97
  384.1 11.6 %fusion.17 = (f32[1024,1792]{1,0:T(8,128)}, f32[1024,1792]{1,0:T(8,128)}) fusion(f32[1024,3584]{1,0:T(8,128)} %fusion.22), kind=kLoop, calls=%fused_computation.34 | loop fusion | bytes 29360128 | tf_op jit(solution)/shard_map/slice | solution.py:107
  395.7 12.3 %reduce-scatter.17.cloned.1.call-done = bf16[24,1024]{1,0:T(8,128)(2,1)} async-done(((bf16[192,1024]{1,0:T(8,128)(2,1)}), bf16[24,1024]{1,0:T(8,128)(2,1)}) %reduce-scatter.17.cloned.1.call-update) | async-done | bytes 49168 | tf_op jit(solution)/shard_map/reduce_scatter | solution.py:98
  (62 shorter events, 14.1 us)
Async XLA Ops:
  7.2 96.6 %reduce-scatter.11.cloned.1.call-start = ((), (), s32[]{:S(2)}) async-start(), calls=%async_computation.9 | async-start | bytes 6881280 | tf_op jit(solution)/shard_map/reduce_scatter | solution.py:43
  38.9 0.8 copy-start.7
  39.0 96.5 %all-gather.3.cloned.1.call-start = ((), (), s32[]{:S(2)}) async-start(), calls=%async_computation.10 | async-start | bytes 1720320 | tf_op jit(solution)/shard_map/all_gather | solution.py:48
  39.7 72.9 %collective-permute-start = (bf16[24,1024]{1,0:T(8,128)(2,1)S(1)}, bf16[24,1024]{1,0:T(8,128)(2,1)S(1)}, u32[]{:S(2)}, u32[]{:S(2)}) collective-permute-start(bf16[24,1024]{1,0:T(8,128)(2,1)S(1)} %copy-done.7), channel_id=1, source_target_pairs={{0,1},{1,2},{2,3},{3,4},{4,5},{5,6},{6,7},{7,0},{8,9},{9,10},{10,1... | collective-permute-start | bytes 147464 | tf_op jit(solution)/shard_map/ppermute | solution.py:13
  40.1 72.6 %collective-permute-start.1 = (bf16[24,1024]{1,0:T(8,128)(2,1)S(1)}, bf16[24,1024]{1,0:T(8,128)(2,1)S(1)}, u32[]{:S(2)}, u32[]{:S(2)}) collective-permute-start(bf16[24,1024]{1,0:T(8,128)(2,1)S(1)} %copy-done.7), channel_id=1, source_target_pairs={{0,7},{1,0},{2,1},{3,2},{4,3},{5,4},{6,5},{7,6},{8,15},{9,8},{10,9... | collective-permute-start | bytes 147464 | tf_op jit(solution)/shard_map/ppermute | solution.py:16
  106.0 73.7 %reduce-scatter.7.cloned.1.call-start = ((), (), s32[]{:S(2)}) async-start(), calls=%async_computation.7 | async-start | bytes 3440640 | tf_op jit(solution)/shard_map/reduce_scatter | solution.py:60
  106.1 4.3 %copy-start.2 = (bf16[1024,1792]{1,0:T(8,128)(2,1)S(1)}, bf16[1024,1792]{1,0:T(8,128)(2,1)}, u32[]{:S(2)}) copy-start(bf16[1024,1792]{1,0:T(8,128)(2,1)} %param.15) | copy-start | bytes 11010052
  112.6 5.5 %collective-permute-start.2 = (bf16[24,1024]{1,0:T(8,128)(2,1)S(1)}, bf16[24,1024]{1,0:T(8,128)(2,1)S(1)}, u32[]{:S(2)}, u32[]{:S(2)}) collective-permute-start(bf16[24,1024]{1,0:T(8,128)(2,1)S(1)} %collective-permute-done), channel_id=1, source_target_pairs={{0,1},{1,2},{2,3},{3,4},{4,5},{5,6},{6,7},{7,0},{8,9},{9,10},{10,1... | collective-permute-start | bytes 147464 | tf_op jit(solution)/shard_map/ppermute | solution.py:13
  112.7 5.4 %collective-permute-start.3 = (bf16[24,1024]{1,0:T(8,128)(2,1)S(1)}, bf16[24,1024]{1,0:T(8,128)(2,1)S(1)}, u32[]{:S(2)}, u32[]{:S(2)}) collective-permute-start(bf16[24,1024]{1,0:T(8,128)(2,1)S(1)} %collective-permute-done.1), channel_id=1, source_target_pairs={{0,7},{1,0},{2,1},{3,2},{4,3},{5,4},{6,5},{7,6},{8,15},{9,8},{10,9... | collective-permute-start | bytes 147464 | tf_op jit(solution)/shard_map/ppermute | solution.py:16
  118.1 5.5 %collective-permute-start.4 = (bf16[24,1024]{1,0:T(8,128)(2,1)S(1)}, bf16[24,1024]{1,0:T(8,128)(2,1)S(1)}, u32[]{:S(2)}, u32[]{:S(2)}) collective-permute-start(bf16[24,1024]{1,0:T(8,128)(2,1)S(1)} %collective-permute-done.2), channel_id=1, source_target_pairs={{0,1},{1,2},{2,3},{3,4},{4,5},{5,6},{6,7},{7,0},{8,9},{9,10},{10,1... | collective-permute-start | bytes 147464 | tf_op jit(solution)/shard_map/ppermute | solution.py:13
  118.1 5.5 %collective-permute-start.5 = (bf16[24,1024]{1,0:T(8,128)(2,1)S(1)}, bf16[24,1024]{1,0:T(8,128)(2,1)S(1)}, u32[]{:S(2)}, u32[]{:S(2)}) collective-permute-start(bf16[24,1024]{1,0:T(8,128)(2,1)S(1)} %collective-permute-done.3), channel_id=1, source_target_pairs={{0,7},{1,0},{2,1},{3,2},{4,3},{5,4},{6,5},{7,6},{8,15},{9,8},{10,9... | collective-permute-start | bytes 147464 | tf_op jit(solution)/shard_map/ppermute | solution.py:16
  123.6 5.3 %collective-permute-start.6 = (bf16[24,1024]{1,0:T(8,128)(2,1)S(1)}, bf16[24,1024]{1,0:T(8,128)(2,1)S(1)}, u32[]{:S(2)}, u32[]{:S(2)}) collective-permute-start(bf16[24,1024]{1,0:T(8,128)(2,1)S(1)} %collective-permute-done.4), channel_id=1, source_target_pairs={{0,1},{1,2},{2,3},{3,4},{4,5},{5,6},{6,7},{7,0},{8,9},{9,10},{10,1... | collective-permute-start | bytes 147464 | tf_op jit(solution)/shard_map/ppermute | solution.py:13
  128.9 6.4 %copy-start = (bf16[192,1024]{1,0:T(8,128)(2,1)}, bf16[192,1024]{1,0:T(8,128)(2,1)S(1)}, u32[]{:S(2)}) copy-start(bf16[192,1024]{1,0:T(8,128)(2,1)S(1)} %constant_dynamic-update-slice_fusion.2) | copy-start | bytes 1179652
  135.3 99.8 %reduce-scatter.13.cloned.1.call-start = ((), (), s32[]{:S(2)}) async-start(), calls=%async_computation.11 | async-start | bytes 1769472 | tf_op jit(solution)/shard_map/reduce_scatter | solution.py:52
  145.2 113.4 %reduce-scatter.9.cloned.1.call-start = ((), (), s32[]{:S(2)}) async-start(), calls=%async_computation.8 | async-start | bytes 983040 | tf_op jit(solution)/shard_map/reduce_scatter | solution.py:68
  235.0 103.6 %reduce-scatter.15.cloned.1.call-start = ((), (), s32[]{:S(2)}) async-start(), calls=%async_computation.12 | async-start | bytes 1720320 | tf_op jit(solution)/shard_map/reduce_scatter | solution.py:83
  269.2 0.7 copy-start.3
  271.7 66.9 %copy-start.5 = (f32[48,3584]{1,0:T(8,128)S(1)}, f32[48,3584]{1,0:T(8,128)}, u32[]{:S(2)}) copy-start(f32[48,3584]{1,0:T(8,128)} %reduce-scatter.7.cloned.1.call-done) | copy-start | bytes 2064388
  306.7 33.8 %copy-start.4 = (bf16[192,1024]{1,0:T(8,128)(2,1)S(1)}, bf16[192,1024]{1,0:T(8,128)(2,1)}, u32[]{:S(2)}) copy-start(bf16[192,1024]{1,0:T(8,128)(2,1)} %copy-done.3) | copy-start | bytes 1179652
  311.3 58.6 %all-gather.5.cloned.1.call-start = ((), (), s32[]{:S(2)}) async-start(), calls=%async_computation.13 | async-start | bytes 1720320 | tf_op jit(solution)/shard_map/all_gather | solution.py:94
  340.5 67.5 %reduce-scatter.17.cloned.1.call-start = ((), (), s32[]{:S(2)}) async-start(), calls=%async_computation.14 | async-start | bytes 442368 | tf_op jit(solution)/shard_map/reduce_scatter | solution.py:98
  352.8 24.0 %copy-start.1 = (bf16[192,1024]{1,0:T(8,128)(2,1)S(1)}, bf16[192,1024]{1,0:T(8,128)(2,1)}, u32[]{:S(2)}) copy-start(bf16[192,1024]{1,0:T(8,128)(2,1)} %copy-done) | copy-start | bytes 1179652
  369.9 6.9 %copy-start.6 = (bf16[192,3584]{1,0:T(8,128)(2,1)S(1)}, bf16[192,3584]{1,0:T(8,128)(2,1)}, u32[]{:S(2)}) copy-start(bf16[192,3584]{1,0:T(8,128)(2,1)} %all-gather.5.cloned.1.call-done) | copy-start | bytes 4128772
Sparse Core Ops, SparseCore 0:
  39.1 64.6 reduce-scatter.10
  106.2 29.1 all-gather.2
  139.0 40.6 reduce-scatter.6
  182.4 36.0 reduce-scatter.12
  235.2 23.4 reduce-scatter.8
  311.4 27.1 reduce-scatter.14
  340.6 29.2 all-gather.4
  376.9 31.0 reduce-scatter.16
